TPU v7x, 1024 devices: a whole 4x4x32 slice. The times are simulated.
1024 devices in a mesh: dp: 32 (over z_lo, core), row: 4 (over x), col: 8 (over y, z_hi).
Axes of the slice: x: 4, y: 4, z: 32 (z_hi: 2, z_lo: 16; z = z_hi * 16 + z_lo), core: 2. Of those that a mesh axis runs over, the one named last changes fastest.
Arguments:
- gate_pre: bfloat16 [4096, 14336], P('dp', 'row'), may hold values from -6 to 6
- up_pre: bfloat16 [4096, 14336], P('dp', 'row'), may hold values from -6 to 6
- down_weight: bfloat16 [14336, 4096], P('row', 'col'), may hold values from -0.046875 to 0.046875
- cotangent: bfloat16 [4096, 4096], P(('dp', 'row'), 'col'), may hold values from -6 to 6
Outputs:
- mixed: bfloat16 [4096, 4096], P(('dp', 'row'), 'col')
- gate_grad: bfloat16 [4096, 14336], P(('dp', 'col'), 'row')
- up_grad: bfloat16 [4096, 14336], P(('dp', 'col'), 'row')
- weight_grad: float32 [14336, 4096], P(('row', 'dp'), 'col')
All inputs are finite; a program needn't handle non-finite values.
Results may differ from a plain program's by a relative error of at most 0.017.
Values may be sent and summed in bfloat16 or wider, within the bound.
A program may use at most 64 MiB of HBM per device.

v0:
```python
import jax
import jax.numpy as jnp
from jax import lax
from jax.sharding import PartitionSpec as P


def body(gate_pre, up_pre, down_weight, cotangent):
    gate_float = gate_pre.astype(jnp.float32)
    up_float = up_pre.astype(jnp.float32)
    sigmoid_gate = jax.nn.sigmoid(gate_float)
    activated = gate_float * sigmoid_gate
    hidden = (activated * up_float).astype(jnp.bfloat16)
    tok_count = hidden.shape[0]
    rows_taken = hidden
    mixed = lax.psum_scatter(
        jnp.dot(rows_taken, down_weight, preferred_element_type=jnp.float32),
        "row",
        scatter_dimension=0,
        tiled=True,
    ).astype(jnp.bfloat16)
    cot_full = lax.all_gather(cotangent, "row", axis=0, tiled=True)
    tok_rows = tok_count // lax.axis_size("col")
    rows_taken = cot_full
    hidden_share = lax.psum_scatter(
        lax.dot_general(
            rows_taken, down_weight, (((1,), (1,)), ((), ())), preferred_element_type=jnp.float32
        ).astype(jnp.bfloat16),
        "col",
        scatter_dimension=0,
        tiled=True,
    ).astype(jnp.float32)
    offset = lax.axis_index("col") * tok_rows
    gate_rows = lax.dynamic_slice_in_dim(gate_float, offset, tok_rows, 0)
    up_rows = lax.dynamic_slice_in_dim(up_float, offset, tok_rows, 0)
    sigmoid_rows = lax.dynamic_slice_in_dim(sigmoid_gate, offset, tok_rows, 0)
    activated_rows = lax.dynamic_slice_in_dim(activated, offset, tok_rows, 0)
    gate_grad = (
        hidden_share * up_rows * sigmoid_rows * (1.0 + gate_rows * (1.0 - sigmoid_rows))
    ).astype(jnp.bfloat16)
    up_grad = (hidden_share * activated_rows).astype(jnp.bfloat16)
    replicas = lax.axis_size("dp")
    grad_total = lax.psum_scatter(
        lax.dot_general(
            hidden, cot_full, (((0,), (0,)), ((), ())), preferred_element_type=jnp.float32
        ),
        "dp",
        scatter_dimension=0,
        tiled=True,
    )
    weight_grad = grad_total / jnp.float32(replicas)
    return (mixed, gate_grad, up_grad, weight_grad)


def solution(mesh):
    placed = (P("dp", "row"), P("dp", "row"), P("row", "col"), P(("dp", "row"), "col"))
    return jax.shard_map(
        body,
        mesh=mesh,
        in_specs=placed,
        out_specs=(
            P(("dp", "row"), "col"),
            P(("dp", "col"), "row"),
            P(("dp", "col"), "row"),
            P(("row", "dp"), "col"),
        ),
        check_vma=False,
    )
```

profile of v0, /device:TPU:6, one launch (start us, length us, event | category | flops | bytes accessed | tf_op | source)
XLA Modules:
  0.0 616.0 jit_solution(4021552621116165648)
XLA Ops:
  7.2 0.0 copy-start.2
  7.2 0.0 reduce-scatter.4.cloned.1.call-start
  7.2 4.1 fusion.5
  11.3 0.0 reduce-scatter.4.cloned.1.call-update
  11.3 0.0 reduce-scatter.6.cloned.1.call-start
  11.4 0.0 copy-done.2
  11.4 21.9 %all_gather.3 = bf16[128,512]{1,0:T(8,128)(2,1)S(1)} all-gather(bf16[32,512]{1,0:T(8,128)(2,1)S(1)} %copy-done.2), channel_id=1, replica_groups=mesh['dp'=32,'row'=4,'col'=8] {'row'}, dimensions={0}, use_global_device_ids=true | all-gather | bytes 163840 | tf_op jit(solution)/shard_map/all_gather | solution.py:21
  33.3 0.0 copy-start
  33.3 0.0 copy-start.1
  33.3 4.5 convolution_convert_fusion
  37.8 0.0 reduce-scatter.6.cloned.1.call-update
  37.8 0.0 reduce-scatter.8.cloned.1.call-start
  37.8 0.0 copy-done
  37.8 0.0 copy-done.1
  37.9 4.1 fusion.4
  42.0 0.0 reduce-scatter.8.cloned.1.call-update
  42.0 1.4 convert_element_type.24
  43.4 1.4 convert_element_type.25
  44.9 1.9 convert_multiply_fusion
  46.8 11.0 %reduce-scatter.4.cloned.1.call-done = f32[32,512]{1,0:T(8,128)} async-done(((f32[128,512]{1,0:T(8,128)}), f32[32,512]{1,0:T(8,128)}) %reduce-scatter.4.cloned.1.call-update) | async-done | bytes 65552 | tf_op jit(solution)/shard_map/reduce_scatter | solution.py:15
  57.8 1.5 convert_element_type.27
  59.2 190.0 %reduce-scatter.6.cloned.1.call-done = bf16[16,3584]{1,0:T(8,128)(2,1)} async-done(((bf16[128,3584]{1,0:T(8,128)(2,1)}), bf16[16,3584]{1,0:T(8,128)(2,1)}) %reduce-scatter.6.cloned.1.call-update) | async-done | bytes 114704 | tf_op jit(solution)/shard_map/reduce_scatter | solution.py:24
  249.2 2.0 fusion.3
  251.2 356.6 %reduce-scatter.8.cloned.1.call-done = f32[112,512]{1,0:T(8,128)} async-done(((f32[3584,512]{1,0:T(8,128)}), f32[112,512]{1,0:T(8,128)}) %reduce-scatter.8.cloned.1.call-update) | async-done | bytes 229392 | tf_op jit(solution)/shard_map/reduce_scatter | solution.py:42
  607.8 1.6 broadcast_multiply_fusion
Async XLA Ops:
  7.2 4.2 copy-start.2
  7.2 50.6 %reduce-scatter.4.cloned.1.call-start = ((), (), s32[]{:S(2)}) async-start(), calls=%async_computation.3 | async-start | bytes 327680 | tf_op jit(solution)/shard_map/reduce_scatter | solution.py:15
  11.3 237.9 %reduce-scatter.6.cloned.1.call-start = ((), (), s32[]{:S(2)}) async-start(), calls=%async_computation.4 | async-start | bytes 1032192 | tf_op jit(solution)/shard_map/reduce_scatter | solution.py:24
  33.3 4.6 copy-start
  33.3 4.6 copy-start.1
  37.8 570.0 %reduce-scatter.8.cloned.1.call-start = ((), (), s32[]{:S(2)}) async-start(), calls=%async_computation.5 | async-start | bytes 7569408 | tf_op jit(solution)/shard_map/reduce_scatter | solution.py:42
Sparse Core Ops, SparseCore 0:
  11.5 46.2 reduce-scatter.3
  64.4 184.7 reduce-scatter.5
  253.1 354.6 reduce-scatter.7
where the time goes:
time: 617 us; the launch traced here: 616 us
  waiting for transfers between devices  558 us (90%)
  blocking collectives  21.9 us (4%)
  between operations  13.8 us (2%)
  matrix products  12.7 us (2%)
  other arithmetic  9.85 us (2%)
    reduce_scatter x1, waiting for transfers between devices, body(): lax.psum_scatter(lax.dot_general(hidden, cot_full, (((0,), (0,)), ((), ()...  357 us
    reduce_scatter x1, waiting for transfers between devices, body(): lax.psum_scatter(lax.dot_general(rows_taken, down_weight, (((1,), (1,)),...  190 us
    all_gather x1, blocking collectives, body(): cot_full = lax.all_gather(cotangent, 'row', axis=0, tiled=True)  21.9 us
  transfers between devices with their start and end apart: 3, of which 3 were waited for; matrix products, arithmetic and copies ran while one was open for 3% of the time, Pallas kernels for 0%

commit v1 on v0

v1 whole, which is shorter than its diff:
```python
import functools

import jax
import jax.numpy as jnp
from jax import lax
from jax.experimental import pallas as pl
from jax.experimental.pallas import tpu as pltpu
from jax.sharding import PartitionSpec as P

F32, BF16 = jnp.float32, jnp.bfloat16
ZL, X, Y = 16, 4, 4
TOK, UNITS, COLS = 128, 3584, 512
OWN = TOK // X
HROWS = TOK // (2 * Y)
CH, NCH = 512, UNITS // 512
SHARD = UNITS // ZL
XB = ((0, 1), (1, 1), (2, 2), (4, 4), (8, 4), (12, 4))


def flip(value, mask):
    out = 0
    for bit in (1, 2, 4, 8):
        have = (value // bit) % 2
        out = out + bit * (1 - have if mask & bit else have)
    return out


def kernel(
    gate, up, w, cot, mixed, gate_grad, up_grad, weight_grad,
    hid, hid_t, cg, hg, part, yrecv, ysum, zsend, zrecv, msend, mrecv, acc, arecv,
    cz_s, cz_r, cx_s, cx_r, h_s, h_r, hy_s, hy_r, p_s, p_r, g_s, g_r, m_s, m_r, a_s, a_r,
):
    dp, row, col = lax.axis_index("dp"), lax.axis_index("row"), lax.axis_index("col")
    zl, core = dp // 2, dp % 2
    y, half = col // 2, col % 2
    z = half * ZL + zl
    slot = (zl % 2) * 8 + ((zl // 2) % 2) * 4 + ((zl // 4) % 2) * 2 + zl // 8

    def at_z(to):
        to = (to + 4 * ZL) % (2 * ZL)
        return {"dp": (to % ZL) * 2 + core, "row": row, "col": y * 2 + to // ZL}

    def at_y(to):
        return {"dp": dp, "row": row, "col": ((to + Y) % Y) * 2 + half}

    def at_x(to):
        return {"dp": dp, "row": (to + X) % X, "col": col}

    other_core = {"dp": zl * 2 + 1 - core, "row": row, "col": col}

    def copy(src, dst, send, recv, to):
        return pltpu.make_async_remote_copy(
            src_ref=src, dst_ref=dst, send_sem=send, recv_sem=recv,
            device_id=to, device_id_type=pl.DeviceIdType.MESH,
        )

    barrier = pltpu.get_barrier_semaphore()

    def greet(to):
        pl.semaphore_signal(barrier, inc=1, device_id=to, device_id_type=pl.DeviceIdType.MESH)

    for e in (1, 2, 3):
        greet(at_x(row + e))
        greet(at_y(y + e))
    greet(other_core)

    @pl.loop(0, 8)
    def _(i):
        greet(at_z(z + 1 + i))
        greet(at_z(z - 1 - i))

    greet(at_z(z + ZL))
    pl.semaphore_wait(barrier, 24)

    mine = pl.ds(pl.multiple_of(row * OWN, OWN), OWN)

    def z_block(q, step):
        block = cg.at[flip(slot, q), mine]
        to = at_z(half * ZL + flip(zl, {1: 8, 2: 4, 4: 2, 8: 1}[step]))
        return copy(block, block, cz_s.at[q + step], cz_r.at[q + step], to)

    def z_arrival(q):
        block = cg.at[flip(slot, q), mine]
        return copy(block, block, cz_s.at[q], cz_r.at[q], at_z(z + 1))

    def x_batch(b, e, frm=None):
        first, count = XB[b]
        start = (flip(slot, first) // count) * count
        rows = mine if frm is None else pl.ds(pl.multiple_of(((frm + X) % X) * OWN, OWN), OWN)
        block = cg.at[pl.ds(start, count), rows]
        i = b * 3 + e - 1
        return copy(block, block, cx_s.at[i], cx_r.at[i], at_x(row + e))

    def forward(b):
        for e in (1, 2, 3):
            x_batch(b, e).start()

    def x_arrivals(b):
        for e in (1, 2, 3):
            x_batch(b, e, row - e).wait_recv()

    cg[slot, mine] = cot[...]
    for step in (1, 2, 4, 8):
        z_block(0, step).start()
    forward(0)

    @pl.loop(0, NCH)
    def _(c):
        at = pl.ds(pl.multiple_of(c * CH, CH), CH)
        g = gate[:, at].astype(F32)
        h = (g * jax.nn.sigmoid(g)) * up[:, at].astype(F32)
        hid[:, at] = h.astype(BF16)
        hid_t[at, :] = h.T.astype(BF16)

    z_arrival(1).wait_recv()
    for step in (2, 4, 8):
        z_block(1, step).start()
    forward(1)

    is_source = zl % Y == y

    def hidden_to(e):
        to = z + e - ZL * (e // 9)
        rows = pl.ds(pl.multiple_of(((zl + e) % ZL) * SHARD, 32), SHARD)
        return copy(hid_t.at[rows], hg.at[slot], h_s.at[e], h_r.at[zl // Y], at_z(to))

    @pl.when(is_source)
    def _():
        @pl.loop(1, ZL)
        def _(e):
            hidden_to(e).start()

    for q in (2, 3):
        z_arrival(q).wait_recv()
        for step in (4, 8):
            z_block(q, step).start()
    forward(2)

    x_arrivals(0)

    def part_copy(c, e):
        rows = pl.ds(pl.multiple_of(((y + e) % Y) * 2 * HROWS, 2 * HROWS), 2 * HROWS)
        i = c * 3 + e - 1
        return copy(part.at[c, rows], yrecv.at[c, e - 1], p_s.at[i], p_r.at[i], at_y(y + e))

    @pl.loop(0, NCH)
    def _(c):
        at = pl.ds(pl.multiple_of(c * CH, CH), CH)
        part[c] = lax.dot_general(
            cg[slot], w[at, :], (((1,), (1,)), ((), ())), preferred_element_type=F32
        ).astype(BF16)
        for e in (1, 2, 3):
            part_copy(c, e).start()

    for q in (4, 5, 6, 7):
        z_arrival(q).wait_recv()
        z_block(q, 8).start()
    forward(3)

    def grad_copy(c):
        return copy(zsend.at[c], zrecv.at[c], g_s.at[c], g_r.at[c], at_z(z + ZL))

    @pl.loop(0, NCH)
    def _(c):
        own = pl.ds(pl.multiple_of(y * 2 * HROWS, 2 * HROWS), 2 * HROWS)
        total = part[c, own].astype(F32)
        for e in (1, 2, 3):
            part_copy(c, e).wait_recv()
            total = total + yrecv[c, e - 1].astype(F32)
        ysum[c, 0] = total[:HROWS]
        ysum[c, 1] = total[HROWS:]
        zsend[c] = ysum[c, 1 - half].astype(BF16)
        grad_copy(c).start()

    turn = (y % 2) * 2 + y // 2

    @pl.when(is_source)
    def _():
        hg[slot] = hid_t[pl.ds(pl.multiple_of(zl * SHARD, 32), SHARD), :]

    @pl.loop(0, ZL // Y)
    def _(m):
        @pl.when(y + Y * m != zl)
        def _():
            copy(hid_t.at[pl.ds(0, SHARD)], hg.at[turn * 4 + (m % 2) * 2 + m // 2], h_s.at[0], h_r.at[m], at_z(z + 1)).wait_recv()

    def hidden_on(e, frm):
        t = (frm % 2) * 2 + frm // 2
        block = hg.at[pl.ds(t * 4, 4)]
        return copy(block, block, hy_s.at[e - 1], hy_r.at[e - 1], at_y(y + e))

    for e in (1, 2, 3):
        hidden_on(e, y).start()

    for b in (4, 5):
        for q in range(XB[b][0], XB[b][0] + 4):
            z_arrival(q).wait_recv()
        forward(b)

    def mixed_copy(e):
        return copy(msend.at[(row + e) % X], mrecv.at[e - 1], m_s.at[e - 1], m_r.at[e - 1], at_x(row + e))

    partial = jnp.dot(hid[...], w[...], preferred_element_type=F32)
    for r in range(X):
        msend[r] = partial[r * OWN : (r + 1) * OWN].astype(BF16)
    for e in (1, 2, 3):
        mixed_copy(e).start()

    for e in (1, 2, 3):
        hidden_on(e, (y - e + Y) % Y).wait_recv()
    for b in range(1, len(XB)):
        x_arrivals(b)

    acc[...] = jnp.zeros_like(acc)

    @pl.loop(0, ZL)
    def _(p):
        product = jnp.dot(hg[p], cg[p], preferred_element_type=F32)
        acc[0] += product[: SHARD // 2]
        acc[1] += product[SHARD // 2 :]

    swap = copy(acc.at[1 - core], arecv, a_s, a_r, other_core)
    swap.start()

    total = msend[row].astype(F32)
    for e in (1, 2, 3):
        mixed_copy(e).wait_recv()
        total = total + mrecv[e - 1].astype(F32)
    mixed[...] = total.astype(BF16)

    swap.wait_recv()
    weight_grad[...] = (acc[core] + arecv[...]) * (1.0 / (2 * ZL))

    @pl.loop(0, NCH)
    def _(c):
        at = pl.ds(pl.multiple_of(c * CH, CH), CH)
        rows = pl.ds(pl.multiple_of(col * HROWS, HROWS), HROWS)
        g = gate[rows, at].astype(F32)
        u = up[rows, at].astype(F32)
        s = jax.nn.sigmoid(g)
        grad_copy(c).wait_recv()
        hidden_grad = ysum[c, half] + zrecv[c].astype(F32)
        gate_grad[:, at] = (hidden_grad * u * s * (1.0 + g * (1.0 - s))).astype(BF16)
        up_grad[:, at] = (hidden_grad * (g * s)).astype(BF16)

    for step in (1, 2, 4, 8):
        for q in range(step):
            z_block(q, step).wait_send()
    for b in range(len(XB)):
        for e in (1, 2, 3):
            x_batch(b, e).wait_send()

    @pl.when(is_source)
    def _():
        @pl.loop(1, ZL)
        def _(e):
            hidden_to(e).wait_send()

    @pl.loop(0, NCH)
    def _(c):
        for e in (1, 2, 3):
            part_copy(c, e).wait_send()
        grad_copy(c).wait_send()

    for e in (1, 2, 3):
        hidden_on(e, y).wait_send()
        mixed_copy(e).wait_send()
    swap.wait_send()


def body(gate_pre, up_pre, down_weight, cotangent):
    vmem = pl.BlockSpec(memory_space=pltpu.VMEM)
    dma = pltpu.SemaphoreType.DMA
    pair = lambda n: [dma((n,)), dma((n,))]
    return pl.pallas_call(
        kernel,
        name="mlp",
        out_shape=(
            jax.ShapeDtypeStruct((OWN, COLS), BF16),
            jax.ShapeDtypeStruct((HROWS, UNITS), BF16),
            jax.ShapeDtypeStruct((HROWS, UNITS), BF16),
            jax.ShapeDtypeStruct((SHARD // 2, COLS), F32),
        ),
        in_specs=[vmem] * 4,
        out_specs=(vmem,) * 4,
        scratch_shapes=[
            pltpu.VMEM((TOK, UNITS), BF16),
            pltpu.VMEM((UNITS, TOK), BF16),
            pltpu.VMEM((ZL, TOK, COLS), BF16),
            pltpu.VMEM((ZL, SHARD, TOK), BF16),
            pltpu.VMEM((NCH, TOK, CH), BF16),
            pltpu.VMEM((NCH, 3, 2 * HROWS, CH), BF16),
            pltpu.VMEM((NCH, 2, HROWS, CH), F32),
            pltpu.VMEM((NCH, HROWS, CH), BF16),
            pltpu.VMEM((NCH, HROWS, CH), BF16),
            pltpu.VMEM((X, OWN, COLS), BF16),
            pltpu.VMEM((3, OWN, COLS), BF16),
            pltpu.VMEM((2, SHARD // 2, COLS), F32),
            pltpu.VMEM((SHARD // 2, COLS), F32),
            *pair(16), *pair(3 * len(XB)), *pair(16), *pair(3), *pair(3 * NCH), *pair(NCH), *pair(3),
            dma, dma,
        ],
        compiler_params=pltpu.CompilerParams(
            collective_id=0, has_side_effects=True, vmem_limit_bytes=40 << 20
        ),
    )(gate_pre, up_pre, down_weight, cotangent)


def solution(mesh):
    placed = (P("dp", "row"), P("dp", "row"), P("row", "col"), P(("dp", "row"), "col"))
    return jax.shard_map(
        body,
        mesh=mesh,
        in_specs=placed,
        out_specs=(
            P(("dp", "row"), "col"),
            P(("dp", "col"), "row"),
            P(("dp", "col"), "row"),
            P(("row", "dp"), "col"),
        ),
        check_vma=False,
    )
```

time: 617 us -> 101 us (0.16)
  the two profiles are of different devices: /device:TPU:6 before, /device:TPU:105 now
where the time goes in v1:
time: 101 us
  Pallas kernels  92.4 us (91%)
  local copies, waits for them, and re-layouts  7.74 us (8%)
    pallas_call x1, Pallas kernels, body(): pl.pallas_call(kernel, name='mlp', out_shape=(jax.ShapeDtypeStruct((OWN,...  92.4 us
    unnamed x12, local copies, waits for them, and re-layouts  7.74 us

profile of v1, /device:TPU:105, one launch (start us, length us, event | category | flops | bytes accessed | tf_op | source)
XLA Modules:
  0.0 100.8 jit_solution(18002232024945272621)
XLA Ops:
  0.6 0.0 copy-start
  0.6 2.0 %copy-done = bf16[3584,512]{1,0:T(8,128)(2,1)S(1)} copy-done((bf16[3584,512]{1,0:T(8,128)(2,1)S(1)}, bf16[3584,512]{1,0:T(8,128)(2,1)}, u32[]{:S(2)}) %copy-start) | copy-done | bytes 3670040
  2.7 0.0 copy-start.1
  2.7 1.2 %copy-done.1 = bf16[128,3584]{1,0:T(8,128)(2,1)S(1)} copy-done((bf16[128,3584]{1,0:T(8,128)(2,1)S(1)}, bf16[128,3584]{1,0:T(8,128)(2,1)}, u32[]{:S(2)}) %copy-start.1) | copy-done | bytes 917528
  3.9 0.0 copy-start.2
  3.9 1.2 %copy-done.2 = bf16[128,3584]{1,0:T(8,128)(2,1)S(1)} copy-done((bf16[128,3584]{1,0:T(8,128)(2,1)S(1)}, bf16[128,3584]{1,0:T(8,128)(2,1)}, u32[]{:S(2)}) %copy-start.2) | copy-done | bytes 917528
  5.0 0.0 copy-start.3
  5.0 0.8 copy-done.3
  5.8 92.4 %mlp.1 = (bf16[32,512]{1,0:T(8,128)(2,1)S(1)}, bf16[16,3584]{1,0:T(8,128)(2,1)S(1)}, bf16[16,3584]{1,0:T(8,128)(2,1)S(1)}, f32[112,512]{1,0:T(8,128)S(1)}) custom-call(bf16[128,3584]{1,0:T(8,128)(2,1)S(1)} %copy-done.1, bf16[128,3584]{1,0:T(8,128)(2,1)S(1)} %copy-done.2, bf16[3584,512]{1,0:T(8,128)(2,1)S(1)} %copy-done, bf16[32,512]{1,0:T(8,128)(2,1)S(1)} %copy-done.3), custom_call_target="tpu_custom_call" | custom-call | tf_op jit(solution)/shard_map/mlp/pallas_call | solution.py:275
  98.2 0.6 copy.12
  98.8 0.6 copy.13
  99.5 0.6 copy.14
  100.1 0.7 copy.15
Async XLA Ops:
  0.6 2.0 %copy-start = (bf16[3584,512]{1,0:T(8,128)(2,1)S(1)}, bf16[3584,512]{1,0:T(8,128)(2,1)}, u32[]{:S(2)}) copy-start(bf16[3584,512]{1,0:T(8,128)(2,1)} %w.1) | copy-start | bytes 11010052
  2.7 1.2 %copy-start.1 = (bf16[128,3584]{1,0:T(8,128)(2,1)S(1)}, bf16[128,3584]{1,0:T(8,128)(2,1)}, u32[]{:S(2)}) copy-start(bf16[128,3584]{1,0:T(8,128)(2,1)} %gate.1) | copy-start | bytes 2752516
  3.9 1.2 %copy-start.2 = (bf16[128,3584]{1,0:T(8,128)(2,1)S(1)}, bf16[128,3584]{1,0:T(8,128)(2,1)}, u32[]{:S(2)}) copy-start(bf16[128,3584]{1,0:T(8,128)(2,1)} %up.1) | copy-start | bytes 2752516
  5.0 0.8 copy-start.3

commit v2 on v1

v2 whole, which is shorter than its diff:
```python
import functools

import jax
import jax.numpy as jnp
from jax import lax
from jax.experimental import pallas as pl
from jax.experimental.pallas import tpu as pltpu
from jax.sharding import PartitionSpec as P

F32, BF16 = jnp.float32, jnp.bfloat16
ZL, X, Y = 16, 4, 4
TOK, UNITS, COLS = 128, 3584, 512
OWN = TOK // X
HROWS = TOK // (2 * Y)
CH, NCH = 512, UNITS // 512
SHARD = UNITS // ZL
PIECE, PAD = SHARD // Y, 64
XB = ((0, 1), (1, 1), (2, 2), (4, 4), (8, 4), (12, 4))
HB = ((4, 8), (0, 4), (12, 4))


def flip(value, mask):
    out = 0
    for bit in (1, 2, 4, 8):
        have = (value // bit) % 2
        out = out + bit * (1 - have if mask & bit else have)
    return out


def kernel(
    gate_in, up_in, w_in, cot_in, mixed_out, gate_grad_out, up_grad_out, weight_grad_out,
    mixed, gate_grad, up_grad, weight_grad, gate_factor, up_factor, gate, up, w, hid, hid_t, cg, hsend, hg, part, yrecv, ysum, zsend, zrecv, msend, mrecv, acc, arecv,
    in_s, out_s, cz_s, cz_r, cx_s, cx_r, h_s, h_r, hy_s, hy_r, p_s, p_r, g_s, g_r, m_s, m_r, a_s, a_r,
):
    dp, row, col = lax.axis_index("dp"), lax.axis_index("row"), lax.axis_index("col")
    zl, core = dp // 2, dp % 2
    y, half = col // 2, col % 2
    z = half * ZL + zl

    def bits_reversed(j):
        return (j % 2) * 8 + ((j // 2) % 2) * 4 + ((j // 4) % 2) * 2 + j // 8

    slot = bits_reversed(zl)
    mine = pl.ds(pl.multiple_of(row * OWN, OWN), OWN)
    load_cot = pltpu.make_async_copy(cot_in, cg.at[slot, mine], in_s.at[0])
    load_w = pltpu.make_async_copy(w_in, w, in_s.at[1])
    load_gate = pltpu.make_async_copy(gate_in, gate, in_s.at[2])
    load_up = pltpu.make_async_copy(up_in, up, in_s.at[3])
    for load in (load_cot, load_gate, load_up, load_w):
        load.start()

    def at_z(to):
        to = (to + 4 * ZL) % (2 * ZL)
        return {"dp": (to % ZL) * 2 + core, "row": row, "col": y * 2 + to // ZL}

    def at_y(to):
        return {"dp": dp, "row": row, "col": ((to + Y) % Y) * 2 + half}

    def at_x(to):
        return {"dp": dp, "row": (to + X) % X, "col": col}

    other_core = {"dp": zl * 2 + 1 - core, "row": row, "col": col}

    def copy(src, dst, send, recv, to):
        return pltpu.make_async_remote_copy(
            src_ref=src, dst_ref=dst, send_sem=send, recv_sem=recv,
            device_id=to, device_id_type=pl.DeviceIdType.MESH,
        )

    barrier = pltpu.get_barrier_semaphore()

    def greet(to):
        pl.semaphore_signal(barrier, inc=1, device_id=to, device_id_type=pl.DeviceIdType.MESH)

    for e in (1, 2, 3):
        greet(at_x(row + e))
        greet(at_y(y + e))
    greet(other_core)

    @pl.loop(0, 8)
    def _(i):
        greet(at_z(z + 1 + i))
        greet(at_z(z - 1 - i))

    load_gate.wait()
    load_up.wait()

    @pl.loop(0, NCH)
    def _(c):
        at = pl.ds(pl.multiple_of(c * CH, CH), CH)
        g = gate[:, at].astype(F32)
        h = (g * jax.nn.sigmoid(g)) * up[:, at].astype(F32)
        hid[:, at] = h.astype(BF16)
        hid_t[at, :] = h.T

    def piece(i):
        rows = pl.ds(pl.multiple_of(i * SHARD + y * PIECE, 8), PIECE)
        return jnp.concatenate([hid_t[rows, :], jnp.zeros((PAD - PIECE, TOK), F32)], axis=0).astype(BF16)

    def piece_to(f):
        return copy(hsend.at[f], hg.at[f, y], h_s.at[f], h_r.at[f], at_z(z + f - 8))

    def send_pieces():
        @pl.loop(0, ZL)
        def _(f):
            @pl.when(f != 8)
            def _():
                piece_to(f).start()

    hg[8, y] = piece(zl)

    @pl.loop(0, ZL)
    def _(f):
        @pl.when(f != 8)
        def _():
            hsend[f] = piece((zl + f + 8) % ZL)

    pl.semaphore_wait(barrier, 23)

    def z_block(q, step):
        block = cg.at[flip(slot, q), mine]
        to = at_z(half * ZL + flip(zl, {1: 8, 2: 4, 4: 2, 8: 1}[step]))
        return copy(block, block, cz_s.at[q + step], cz_r.at[q + step], to)

    def z_arrival(q):
        block = cg.at[flip(slot, q), mine]
        return copy(block, block, cz_s.at[q], cz_r.at[q], at_z(z + 1))

    def x_batch(b, e, frm=None):
        first, count = XB[b]
        start = (flip(slot, first) // count) * count
        rows = mine if frm is None else pl.ds(pl.multiple_of(((frm + X) % X) * OWN, OWN), OWN)
        block = cg.at[pl.ds(start, count), rows]
        i = b * 3 + e - 1
        return copy(block, block, cx_s.at[i], cx_r.at[i], at_x(row + e))

    def forward(b):
        for e in (1, 2, 3):
            x_batch(b, e).start()

    def x_arrivals(b):
        for e in (1, 2, 3):
            x_batch(b, e, row - e).wait_recv()

    load_cot.wait()
    forward(0)
    for step in (1, 2, 4, 8):
        z_block(0, step).start()

    send_pieces()

    def part_copy(c, e):
        rows = pl.ds(pl.multiple_of(((y + e) % Y) * 2 * HROWS, 2 * HROWS), 2 * HROWS)
        i = c * 3 + e - 1
        return copy(part.at[c, rows], yrecv.at[c, e - 1], p_s.at[i], p_r.at[i], at_y(y + e))

    def part_chunks(first, last):
        @pl.loop(first, last)
        def _(c):
            at = pl.ds(pl.multiple_of(c * CH, CH), CH)
            part[c] = lax.dot_general(
                cg[slot], w[at, :], (((1,), (1,)), ((), ())), preferred_element_type=F32
            ).astype(BF16)
            for e in (1, 2, 3):
                part_copy(c, e).start()

    load_w.wait()
    x_arrivals(0)
    part_chunks(0, 1)
    z_arrival(1).wait_recv()
    for step in (2, 4, 8):
        z_block(1, step).start()
    forward(1)
    part_chunks(1, 4)
    for q in (2, 3):
        z_arrival(q).wait_recv()
        for step in (4, 8):
            z_block(q, step).start()
    forward(2)
    part_chunks(4, NCH)

    def grad_copy(c):
        return copy(zsend.at[c], zrecv.at[c], g_s.at[c], g_r.at[c], at_z(z + ZL))

    def sum_chunks(first, last):
        @pl.loop(first, last)
        def _(c):
            own = pl.ds(pl.multiple_of(y * 2 * HROWS, 2 * HROWS), 2 * HROWS)
            total = part[c, own].astype(F32)
            for e in (1, 2, 3):
                part_copy(c, e).wait_recv()
                total = total + yrecv[c, e - 1].astype(F32)
            ysum[c, 0] = total[:HROWS]
            ysum[c, 1] = total[HROWS:]
            zsend[c] = ysum[c, 1 - half].astype(BF16)
            grad_copy(c).start()

    sum_chunks(0, 3)
    for q in (4, 5, 6, 7):
        z_arrival(q).wait_recv()
        z_block(q, 8).start()
    forward(3)
    sum_chunks(3, NCH)


    def mixed_copy(e):
        return copy(msend.at[(row + e) % X], mrecv.at[e - 1], m_s.at[e - 1], m_r.at[e - 1], at_x(row + e))

    partial = jnp.dot(hid[...], w[...], preferred_element_type=F32)
    for r in range(X):
        msend[r] = partial[r * OWN : (r + 1) * OWN].astype(BF16)
    for e in (1, 2, 3):
        mixed_copy(e).start()

    @pl.loop(0, NCH)
    def _(c):
        at = pl.ds(pl.multiple_of(c * CH, CH), CH)
        rows = pl.ds(pl.multiple_of(col * HROWS, HROWS), HROWS)
        g = gate[rows, at].astype(F32)
        sg = jax.nn.sigmoid(g)
        gate_factor[c] = up[rows, at].astype(F32) * sg * (1.0 + g * (1.0 - sg))
        up_factor[c] = g * sg

    def piece_on(b, e, frm):
        first, count = HB[b]
        block = hg.at[pl.ds(first, count), frm]
        i = b * 3 + e - 1
        return copy(block, block, hy_s.at[i], hy_r.at[i], at_y(y + e))

    for b, (first, count) in enumerate(HB):
        for f in range(first, first + count):
            if f != 8:
                piece_to(f).wait_recv()
        for e in (1, 2, 3):
            piece_on(b, e, y).start()

    for b in (4, 5):
        for q in range(XB[b][0], XB[b][0] + 4):
            z_arrival(q).wait_recv()
        forward(b)

    for b in range(len(HB)):
        for e in (1, 2, 3):
            piece_on(b, e, (y - e + Y) % Y).wait_recv()
    for b in range(1, len(XB)):
        x_arrivals(b)

    acc[...] = jnp.zeros_like(acc)

    @pl.loop(0, ZL)
    def _(f):
        product = jnp.dot(
            hg[f].reshape(Y * PAD, TOK), cg[bits_reversed((zl + 8 - f + ZL) % ZL)], preferred_element_type=F32
        )
        for q in range(Y):
            acc[q // 2, (q % 2) * PIECE : (q % 2 + 1) * PIECE] += product[q * PAD : q * PAD + PIECE]

    swap = copy(acc.at[1 - core], arecv, a_s, a_r, other_core)
    swap.start()

    total = msend[row].astype(F32)
    for e in (1, 2, 3):
        mixed_copy(e).wait_recv()
        total = total + mrecv[e - 1].astype(F32)
    mixed[...] = total.astype(BF16)
    store_mixed = pltpu.make_async_copy(mixed, mixed_out, out_s.at[0])
    store_mixed.start()

    swap.wait_recv()
    weight_grad[...] = (acc[core] + arecv[...]) * (1.0 / (2 * ZL))
    store_weight = pltpu.make_async_copy(weight_grad, weight_grad_out, out_s.at[1])
    store_weight.start()

    @pl.loop(0, NCH)
    def _(c):
        at = pl.ds(pl.multiple_of(c * CH, CH), CH)
        grad_copy(c).wait_recv()
        hidden_grad = ysum[c, half] + zrecv[c].astype(F32)
        gate_grad[:, at] = (hidden_grad * gate_factor[c]).astype(BF16)
        up_grad[:, at] = (hidden_grad * up_factor[c]).astype(BF16)

    store_gate = pltpu.make_async_copy(gate_grad, gate_grad_out, out_s.at[2])
    store_up = pltpu.make_async_copy(up_grad, up_grad_out, out_s.at[3])
    store_gate.start()
    store_up.start()

    for step in (1, 2, 4, 8):
        for q in range(step):
            z_block(q, step).wait_send()
    for b in range(len(XB)):
        for e in (1, 2, 3):
            x_batch(b, e).wait_send()

    @pl.loop(0, ZL)
    def _(f):
        @pl.when(f != 8)
        def _():
            piece_to(f).wait_send()

    @pl.loop(0, NCH)
    def _(c):
        for e in (1, 2, 3):
            part_copy(c, e).wait_send()
        grad_copy(c).wait_send()

    for e in (1, 2, 3):
        for b in range(len(HB)):
            piece_on(b, e, y).wait_send()
        mixed_copy(e).wait_send()
    swap.wait_send()
    for store in (store_mixed, store_weight, store_gate, store_up):
        store.wait()


def body(gate_pre, up_pre, down_weight, cotangent):
    hbm = pl.BlockSpec(memory_space=pltpu.HBM)
    dma = pltpu.SemaphoreType.DMA
    pair = lambda n: [dma((n,)), dma((n,))]
    return pl.pallas_call(
        kernel,
        name="mlp",
        out_shape=(
            jax.ShapeDtypeStruct((OWN, COLS), BF16),
            jax.ShapeDtypeStruct((HROWS, UNITS), BF16),
            jax.ShapeDtypeStruct((HROWS, UNITS), BF16),
            jax.ShapeDtypeStruct((SHARD // 2, COLS), F32),
        ),
        in_specs=[hbm] * 4,
        out_specs=(hbm,) * 4,
        scratch_shapes=[
            pltpu.VMEM((OWN, COLS), BF16),
            pltpu.VMEM((HROWS, UNITS), BF16),
            pltpu.VMEM((HROWS, UNITS), BF16),
            pltpu.VMEM((SHARD // 2, COLS), F32),
            pltpu.VMEM((NCH, HROWS, CH), F32),
            pltpu.VMEM((NCH, HROWS, CH), F32),
            pltpu.VMEM((TOK, UNITS), BF16),
            pltpu.VMEM((TOK, UNITS), BF16),
            pltpu.VMEM((UNITS, COLS), BF16),
            pltpu.VMEM((TOK, UNITS), BF16),
            pltpu.VMEM((UNITS, TOK), F32),
            pltpu.VMEM((ZL, TOK, COLS), BF16),
            pltpu.VMEM((ZL, PAD, TOK), BF16),
            pltpu.VMEM((ZL, Y, PAD, TOK), BF16),
            pltpu.VMEM((NCH, TOK, CH), BF16),
            pltpu.VMEM((NCH, 3, 2 * HROWS, CH), BF16),
            pltpu.VMEM((NCH, 2, HROWS, CH), F32),
            pltpu.VMEM((NCH, HROWS, CH), BF16),
            pltpu.VMEM((NCH, HROWS, CH), BF16),
            pltpu.VMEM((X, OWN, COLS), BF16),
            pltpu.VMEM((3, OWN, COLS), BF16),
            pltpu.VMEM((2, SHARD // 2, COLS), F32),
            pltpu.VMEM((SHARD // 2, COLS), F32),
            dma((4,)), dma((4,)), *pair(16), *pair(3 * len(XB)), *pair(ZL), *pair(3 * len(HB)), *pair(3 * NCH), *pair(NCH), *pair(3),
            dma, dma,
        ],
        compiler_params=pltpu.CompilerParams(
            collective_id=0, has_side_effects=True, vmem_limit_bytes=60 << 20
        ),
    )(gate_pre, up_pre, down_weight, cotangent)


def solution(mesh):
    placed = (P("dp", "row"), P("dp", "row"), P("row", "col"), P(("dp", "row"), "col"))
    return jax.shard_map(
        body,
        mesh=mesh,
        in_specs=placed,
        out_specs=(
            P(("dp", "row"), "col"),
            P(("dp", "col"), "row"),
            P(("dp", "col"), "row"),
            P(("row", "dp"), "col"),
        ),
        check_vma=False,
    )
```

time: 101 us -> 85.8 us (0.85)
  the two profiles are of different devices: /device:TPU:105 before, /device:TPU:1 now
where the time goes in v2:
time: 85.8 us; the launch traced here: 85.5 us
  Pallas kernels  78.7 us (92%)
  local copies, waits for them, and re-layouts  6.12 us (7%)
    pallas_call x1, Pallas kernels, body(): pl.pallas_call(kernel, name='mlp', out_shape=(jax.ShapeDtypeStruct((OWN,...  78.7 us
    unnamed x4, local copies, waits for them, and re-layouts  6.12 us

profile of v2, /device:TPU:1, one launch (start us, length us, event | category | flops | bytes accessed | tf_op | source)
XLA Modules:
  0.0 85.5 jit_solution(16545951573666595230)
XLA Ops:
  0.6 78.7 %mlp.1 = (bf16[32,512]{1,0:T(8,128)(2,1)}, bf16[16,3584]{1,0:T(8,128)(2,1)}, bf16[16,3584]{1,0:T(8,128)(2,1)}, f32[112,512]{1,0:T(8,128)}) custom-call(bf16[128,3584]{1,0:T(8,128)(2,1)} %gate_in.1, bf16[128,3584]{1,0:T(8,128)(2,1)} %up_in.1, bf16[3584,512]{1,0:T(8,128)(2,1)} %w_in.1, bf16[32,512]{1,0:T(8,128)(2,1)} %cot_in.1), custom_call_target="tpu_custom_call" | custom-call | tf_op jit(solution)/shard_map/mlp/pallas_call | solution.py:319
  79.4 1.4 %copy.12 = bf16[32,512]{1,0:T(8,128)(2,1)} copy(bf16[32,512]{1,0:T(8,128)(2,1)} %get-tuple-element.8) | data formatting | bytes 65536
  80.7 1.6 %copy.13 = bf16[16,3584]{1,0:T(8,128)(2,1)} copy(bf16[16,3584]{1,0:T(8,128)(2,1)} %get-tuple-element.9) | data formatting | bytes 229376
  82.3 1.6 %copy.14 = bf16[16,3584]{1,0:T(8,128)(2,1)} copy(bf16[16,3584]{1,0:T(8,128)(2,1)} %get-tuple-element.10) | data formatting | bytes 229376
  83.8 1.6 %copy.15 = f32[112,512]{1,0:T(8,128)} copy(f32[112,512]{1,0:T(8,128)} %get-tuple-element.11) | data formatting | bytes 458752

commit v3 on v2

--- a/solution.py
+++ b/solution.py
@@ -14,9 +14,10 @@
 HROWS = TOK // (2 * Y)
 CH, NCH = 512, UNITS // 512
 SHARD = UNITS // ZL
-PIECE, PAD = SHARD // Y, 64
-XB = ((0, 1), (1, 1), (2, 2), (4, 4), (8, 4), (12, 4))
-HB = ((4, 8), (0, 4), (12, 4))
+PIECE = 2 * SHARD // Y
+NT = ZL // 2
+XB = ((0, 1), (1, 1), (2, 2), (4, 2), (6, 2))
+HB = ((2, 4), (0, 2), (6, 2))
 
 
 def flip(value, mask):
@@ -29,18 +30,18 @@
 
 def kernel(
     gate_in, up_in, w_in, cot_in, mixed_out, gate_grad_out, up_grad_out, weight_grad_out,
-    mixed, gate_grad, up_grad, weight_grad, gate_factor, up_factor, gate, up, w, hid, hid_t, cg, hsend, hg, part, yrecv, ysum, zsend, zrecv, msend, mrecv, acc, arecv,
-    in_s, out_s, cz_s, cz_r, cx_s, cx_r, h_s, h_r, hy_s, hy_r, p_s, p_r, g_s, g_r, m_s, m_r, a_s, a_r,
+    mixed, gate_grad, up_grad, weight_grad, gate_factor, up_factor, gate, up, w, hid, hid_t, cg, hg, part, yrecv, ysum, zsend, zrecv, msend, mrecv, acc, arecv, nsend, nrecv,
+    in_s, out_s, cz_s, cz_r, cx_s, cx_r, h_s, h_r, hy_s, hy_r, p_s, p_r, g_s, g_r, m_s, m_r, a_s, a_r, n_s, n_r,
 ):
     dp, row, col = lax.axis_index("dp"), lax.axis_index("row"), lax.axis_index("col")
     zl, core = dp // 2, dp % 2
     y, half = col // 2, col % 2
     z = half * ZL + zl
 
-    def bits_reversed(j):
-        return (j % 2) * 8 + ((j // 2) % 2) * 4 + ((j // 4) % 2) * 2 + j // 8
-
-    slot = bits_reversed(zl)
+    def slot_of(j):
+        return ((j // 2) % 2) * 4 + ((j // 4) % 2) * 2 + j // 8
+
+    slot = slot_of(zl)
     mine = pl.ds(pl.multiple_of(row * OWN, OWN), OWN)
     load_cot = pltpu.make_async_copy(cot_in, cg.at[slot, mine], in_s.at[0])
     load_w = pltpu.make_async_copy(w_in, w, in_s.at[1])
@@ -60,6 +61,9 @@
         return {"dp": dp, "row": (to + X) % X, "col": col}
 
     other_core = {"dp": zl * 2 + 1 - core, "row": row, "col": col}
+    odd = zl % 2
+    next_zl = flip(zl, 1)
+    next_chip = ({"dp": next_zl * 2 + core, "row": row, "col": col}, {"dp": next_zl * 2 + 1 - core, "row": row, "col": col})
 
     def copy(src, dst, send, recv, to):
         return pltpu.make_async_remote_copy(
@@ -76,11 +80,13 @@
         greet(at_x(row + e))
         greet(at_y(y + e))
     greet(other_core)
-
-    @pl.loop(0, 8)
+    greet(next_chip[0])
+    greet(next_chip[1])
+
+    @pl.loop(1, 5)
     def _(i):
-        greet(at_z(z + 1 + i))
-        greet(at_z(z - 1 - i))
+        greet(at_z(z + 2 * i))
+        greet(at_z(z - 2 * i))
 
     load_gate.wait()
     load_up.wait()
@@ -91,35 +97,29 @@
         g = gate[:, at].astype(F32)
         h = (g * jax.nn.sigmoid(g)) * up[:, at].astype(F32)
         hid[:, at] = h.astype(BF16)
-        hid_t[at, :] = h.T
+        hid_t[at, :] = h.T.astype(BF16)
 
     def piece(i):
-        rows = pl.ds(pl.multiple_of(i * SHARD + y * PIECE, 8), PIECE)
-        return jnp.concatenate([hid_t[rows, :], jnp.zeros((PAD - PIECE, TOK), F32)], axis=0).astype(BF16)
-
-    def piece_to(f):
-        return copy(hsend.at[f], hg.at[f, y], h_s.at[f], h_r.at[f], at_z(z + f - 8))
+        return pl.ds(pl.multiple_of((i // 2) * 2 * SHARD + y * PIECE, 16), PIECE)
+
+    def piece_to(g):
+        rows = piece((zl + 2 * g + 8) % ZL)
+        far = (1 - jnp.minimum(g, 1)) * ((zl // 2) % 2) * ZL
+        return copy(hid_t.at[rows], hg.at[g, y], h_s.at[g], h_r.at[g], at_z(z + 2 * g - 8 + far))
 
     def send_pieces():
-        @pl.loop(0, ZL)
-        def _(f):
-            @pl.when(f != 8)
+        @pl.loop(0, NT)
+        def _(g):
+            @pl.when(g != 4)
             def _():
-                piece_to(f).start()
-
-    hg[8, y] = piece(zl)
-
-    @pl.loop(0, ZL)
-    def _(f):
-        @pl.when(f != 8)
-        def _():
-            hsend[f] = piece((zl + f + 8) % ZL)
-
-    pl.semaphore_wait(barrier, 23)
+                piece_to(g).start()
+
+    hg[4, y] = hid_t[piece(zl), :]
+    pl.semaphore_wait(barrier, 17)
 
     def z_block(q, step):
         block = cg.at[flip(slot, q), mine]
-        to = at_z(half * ZL + flip(zl, {1: 8, 2: 4, 4: 2, 8: 1}[step]))
+        to = at_z(half * ZL + flip(zl, {1: 8, 2: 4, 4: 2}[step]))
         return copy(block, block, cz_s.at[q + step], cz_r.at[q + step], to)
 
     def z_arrival(q):
@@ -144,7 +144,7 @@
 
     load_cot.wait()
     forward(0)
-    for step in (1, 2, 4, 8):
+    for step in (1, 2, 4):
         z_block(0, step).start()
 
     send_pieces()
@@ -163,21 +163,6 @@
             ).astype(BF16)
             for e in (1, 2, 3):
                 part_copy(c, e).start()
-
-    load_w.wait()
-    x_arrivals(0)
-    part_chunks(0, 1)
-    z_arrival(1).wait_recv()
-    for step in (2, 4, 8):
-        z_block(1, step).start()
-    forward(1)
-    part_chunks(1, 4)
-    for q in (2, 3):
-        z_arrival(q).wait_recv()
-        for step in (4, 8):
-            z_block(q, step).start()
-    forward(2)
-    part_chunks(4, NCH)
 
     def grad_copy(c):
         return copy(zsend.at[c], zrecv.at[c], g_s.at[c], g_r.at[c], at_z(z + ZL))
@@ -195,13 +180,42 @@
             zsend[c] = ysum[c, 1 - half].astype(BF16)
             grad_copy(c).start()
 
-    sum_chunks(0, 3)
-    for q in (4, 5, 6, 7):
-        z_arrival(q).wait_recv()
-        z_block(q, 8).start()
+    def pass_on(blocks):
+        for q in blocks:
+            z_arrival(q).wait_recv()
+            for step in (1, 2, 4):
+                if step > q:
+                    z_block(q, step).start()
+
+    def piece_on(b, e, frm):
+        first, count = HB[b]
+        block = hg.at[pl.ds(first, count), frm]
+        i = b * 3 + e - 1
+        return copy(block, block, hy_s.at[i], hy_r.at[i], at_y(y + e))
+
+    def pieces_on(b):
+        first, count = HB[b]
+        for f in range(first, first + count):
+            if f != 4:
+                piece_to(f).wait_recv()
+        for e in (1, 2, 3):
+            piece_on(b, e, y).start()
+
+    pass_on((1, 2, 4))
+    forward(1)
+    load_w.wait()
+    x_arrivals(0)
+    part_chunks(0, NCH)
+    pass_on((3,))
+    forward(2)
+    pass_on((5,))
     forward(3)
-    sum_chunks(3, NCH)
-
+    pass_on((6, 7))
+    forward(4)
+    pieces_on(0)
+    pieces_on(1)
+    pieces_on(2)
+    sum_chunks(0, NCH)
 
     def mixed_copy(e):
         return copy(msend.at[(row + e) % X], mrecv.at[e - 1], m_s.at[e - 1], m_r.at[e - 1], at_x(row + e))
@@ -221,40 +235,34 @@
         gate_factor[c] = up[rows, at].astype(F32) * sg * (1.0 + g * (1.0 - sg))
         up_factor[c] = g * sg
 
-    def piece_on(b, e, frm):
-        first, count = HB[b]
-        block = hg.at[pl.ds(first, count), frm]
-        i = b * 3 + e - 1
-        return copy(block, block, hy_s.at[i], hy_r.at[i], at_y(y + e))
-
-    for b, (first, count) in enumerate(HB):
-        for f in range(first, first + count):
-            if f != 8:
-                piece_to(f).wait_recv()
-        for e in (1, 2, 3):
-            piece_on(b, e, y).start()
-
-    for b in (4, 5):
-        for q in range(XB[b][0], XB[b][0] + 4):
-            z_arrival(q).wait_recv()
-        forward(b)
-
     for b in range(len(HB)):
         for e in (1, 2, 3):
             piece_on(b, e, (y - e + Y) % Y).wait_recv()
     for b in range(1, len(XB)):
         x_arrivals(b)
 
-    acc[...] = jnp.zeros_like(acc)
-
-    @pl.loop(0, ZL)
-    def _(f):
-        product = jnp.dot(
-            hg[f].reshape(Y * PAD, TOK), cg[bits_reversed((zl + 8 - f + ZL) % ZL)], preferred_element_type=F32
-        )
-        for q in range(Y):
-            acc[q // 2, (q % 2) * PIECE : (q % 2 + 1) * PIECE] += product[q * PAD : q * PAD + PIECE]
-
+    def sums(chip):
+        acc[...] = jnp.zeros_like(acc)
+
+        @pl.loop(0, NT)
+        def _(g):
+            product = jnp.dot(
+                hg[g, pl.ds(chip * 2, 2)].reshape(SHARD, TOK),
+                cg[slot_of((zl + 8 - 2 * g + ZL) % ZL)],
+                preferred_element_type=F32,
+            )
+            acc[0] += product[:PIECE]
+            acc[1] += product[PIECE:]
+
+    def chip_copy(k):
+        return copy(nsend.at[k], nrecv.at[k], n_s.at[k], n_r.at[k], next_chip[k])
+
+    sums(1 - odd)
+    nsend[0] = acc[core].astype(BF16)
+    nsend[1] = acc[1 - core].astype(BF16)
+    chip_copy(0).start()
+    chip_copy(1).start()
+    sums(odd)
     swap = copy(acc.at[1 - core], arecv, a_s, a_r, other_core)
     swap.start()
 
@@ -267,7 +275,11 @@
     store_mixed.start()
 
     swap.wait_recv()
-    weight_grad[...] = (acc[core] + arecv[...]) * (1.0 / (2 * ZL))
+    total = acc[core] + arecv[...]
+    for k in (0, 1):
+        chip_copy(k).wait_recv()
+        total = total + nrecv[k].astype(F32)
+    weight_grad[...] = total * (1.0 / (2 * ZL))
     store_weight = pltpu.make_async_copy(weight_grad, weight_grad_out, out_s.at[1])
     store_weight.start()
 
@@ -284,18 +296,18 @@
     store_gate.start()
     store_up.start()
 
-    for step in (1, 2, 4, 8):
+    for step in (1, 2, 4):
         for q in range(step):
             z_block(q, step).wait_send()
     for b in range(len(XB)):
         for e in (1, 2, 3):
             x_batch(b, e).wait_send()
 
-    @pl.loop(0, ZL)
-    def _(f):
-        @pl.when(f != 8)
+    @pl.loop(0, NT)
+    def _(g):
+        @pl.when(g != 4)
         def _():
-            piece_to(f).wait_send()
+            piece_to(g).wait_send()
 
     @pl.loop(0, NCH)
     def _(c):
@@ -308,6 +320,8 @@
             piece_on(b, e, y).wait_send()
         mixed_copy(e).wait_send()
     swap.wait_send()
+    for k in (0, 1):
+        chip_copy(k).wait_send()
     for store in (store_mixed, store_weight, store_gate, store_up):
         store.wait()
 
@@ -338,10 +352,9 @@
             pltpu.VMEM((TOK, UNITS), BF16),
             pltpu.VMEM((UNITS, COLS), BF16),
             pltpu.VMEM((TOK, UNITS), BF16),
-            pltpu.VMEM((UNITS, TOK), F32),
-            pltpu.VMEM((ZL, TOK, COLS), BF16),
-            pltpu.VMEM((ZL, PAD, TOK), BF16),
-            pltpu.VMEM((ZL, Y, PAD, TOK), BF16),
+            pltpu.VMEM((UNITS, TOK), BF16),
+            pltpu.VMEM((NT, TOK, COLS), BF16),
+            pltpu.VMEM((NT, Y, PIECE, TOK), BF16),
             pltpu.VMEM((NCH, TOK, CH), BF16),
             pltpu.VMEM((NCH, 3, 2 * HROWS, CH), BF16),
             pltpu.VMEM((NCH, 2, HROWS, CH), F32),
@@ -351,8 +364,10 @@
             pltpu.VMEM((3, OWN, COLS), BF16),
             pltpu.VMEM((2, SHARD // 2, COLS), F32),
             pltpu.VMEM((SHARD // 2, COLS), F32),
-            dma((4,)), dma((4,)), *pair(16), *pair(3 * len(XB)), *pair(ZL), *pair(3 * len(HB)), *pair(3 * NCH), *pair(NCH), *pair(3),
-            dma, dma,
+            pltpu.VMEM((2, SHARD // 2, COLS), BF16),
+            pltpu.VMEM((2, SHARD // 2, COLS), BF16),
+            dma((4,)), dma((4,)), *pair(NT), *pair(3 * len(XB)), *pair(NT), *pair(3 * len(HB)), *pair(3 * NCH), *pair(NCH), *pair(3),
+            dma, dma, *pair(2),
         ],
         compiler_params=pltpu.CompilerParams(
             collective_id=0, has_side_effects=True, vmem_limit_bytes=60 << 20

time: 85.8 us -> 82.4 us (0.960)
  Pallas kernels: 78.7 us -> 75.4 us
    pallas_call x1, Pallas kernels: 78.7 us -> 75.4 us  [body(): pl.pallas_call(kernel, name='mlp', out_shape=(jax.ShapeDtypeStruct((OWN,...]
where the time goes in v3:
time: 82.4 us; the launch traced here: 82.1 us
  Pallas kernels  75.4 us (92%)
  local copies, waits for them, and re-layouts  6.12 us (7%)
    pallas_call x1, Pallas kernels, body(): pl.pallas_call(kernel, name='mlp', out_shape=(jax.ShapeDtypeStruct((OWN,...  75.4 us
    unnamed x4, local copies, waits for them, and re-layouts  6.12 us

profile of v3, /device:TPU:1, one launch (start us, length us, event | category | flops | bytes accessed | tf_op | source)
XLA Modules:
  0.0 82.1 jit_solution(9956109840753311430)
XLA Ops:
  0.6 75.4 %mlp.1 = (bf16[32,512]{1,0:T(8,128)(2,1)}, bf16[16,3584]{1,0:T(8,128)(2,1)}, bf16[16,3584]{1,0:T(8,128)(2,1)}, f32[112,512]{1,0:T(8,128)}) custom-call(bf16[128,3584]{1,0:T(8,128)(2,1)} %gate_in.1, bf16[128,3584]{1,0:T(8,128)(2,1)} %up_in.1, bf16[3584,512]{1,0:T(8,128)(2,1)} %w_in.1, bf16[32,512]{1,0:T(8,128)(2,1)} %cot_in.1), custom_call_target="tpu_custom_call" | custom-call | tf_op jit(solution)/shard_map/mlp/pallas_call | solution.py:333
  76.0 1.4 %copy.12 = bf16[32,512]{1,0:T(8,128)(2,1)} copy(bf16[32,512]{1,0:T(8,128)(2,1)} %get-tuple-element.8) | data formatting | bytes 65536
  77.4 1.6 %copy.13 = bf16[16,3584]{1,0:T(8,128)(2,1)} copy(bf16[16,3584]{1,0:T(8,128)(2,1)} %get-tuple-element.9) | data formatting | bytes 229376
  78.9 1.6 %copy.14 = bf16[16,3584]{1,0:T(8,128)(2,1)} copy(bf16[16,3584]{1,0:T(8,128)(2,1)} %get-tuple-element.10) | data formatting | bytes 229376
  80.5 1.6 %copy.15 = f32[112,512]{1,0:T(8,128)} copy(f32[112,512]{1,0:T(8,128)} %get-tuple-element.11) | data formatting | bytes 458752

commit v4 on v3

--- a/solution.py
+++ b/solution.py
@@ -29,9 +29,9 @@
 
 
 def kernel(
-    gate_in, up_in, w_in, cot_in, mixed_out, gate_grad_out, up_grad_out, weight_grad_out,
-    mixed, gate_grad, up_grad, weight_grad, gate_factor, up_factor, gate, up, w, hid, hid_t, cg, hg, part, yrecv, ysum, zsend, zrecv, msend, mrecv, acc, arecv, nsend, nrecv,
-    in_s, out_s, cz_s, cz_r, cx_s, cx_r, h_s, h_r, hy_s, hy_r, p_s, p_r, g_s, g_r, m_s, m_r, a_s, a_r, n_s, n_r,
+    gate_in, up_in, w_in, cot_in, mixed, gate_grad, up_grad, weight_grad,
+    gate_factor, up_factor, gate, up, w, hid, hid_t, cg, hg, part, yrecv, ysum, zsend, zrecv, msend, mrecv, acc, arecv, nsend, nrecv,
+    in_s, cz_s, cz_r, cx_s, cx_r, h_s, h_r, hy_s, hy_r, p_s, p_r, g_s, g_r, m_s, m_r, a_s, a_r, n_s, n_r,
 ):
     dp, row, col = lax.axis_index("dp"), lax.axis_index("row"), lax.axis_index("col")
     zl, core = dp // 2, dp % 2
@@ -271,8 +271,6 @@
         mixed_copy(e).wait_recv()
         total = total + mrecv[e - 1].astype(F32)
     mixed[...] = total.astype(BF16)
-    store_mixed = pltpu.make_async_copy(mixed, mixed_out, out_s.at[0])
-    store_mixed.start()
 
     swap.wait_recv()
     total = acc[core] + arecv[...]
@@ -280,8 +278,6 @@
         chip_copy(k).wait_recv()
         total = total + nrecv[k].astype(F32)
     weight_grad[...] = total * (1.0 / (2 * ZL))
-    store_weight = pltpu.make_async_copy(weight_grad, weight_grad_out, out_s.at[1])
-    store_weight.start()
 
     @pl.loop(0, NCH)
     def _(c):
@@ -291,11 +287,6 @@
         gate_grad[:, at] = (hidden_grad * gate_factor[c]).astype(BF16)
         up_grad[:, at] = (hidden_grad * up_factor[c]).astype(BF16)
 
-    store_gate = pltpu.make_async_copy(gate_grad, gate_grad_out, out_s.at[2])
-    store_up = pltpu.make_async_copy(up_grad, up_grad_out, out_s.at[3])
-    store_gate.start()
-    store_up.start()
-
     for step in (1, 2, 4):
         for q in range(step):
             z_block(q, step).wait_send()
@@ -322,30 +313,37 @@
     swap.wait_send()
     for k in (0, 1):
         chip_copy(k).wait_send()
-    for store in (store_mixed, store_weight, store_gate, store_up):
-        store.wait()
+
+
+def hand_over(a, b, c, d, a_out, b_out, c_out, d_out, sems):
+    copies = [
+        pltpu.make_async_copy(src, dst, sems.at[i])
+        for i, (src, dst) in enumerate(((a, a_out), (b, b_out), (c, c_out), (d, d_out)))
+    ]
+    for c in copies:
+        c.start()
+    for c in copies:
+        c.wait()
 
 
 def body(gate_pre, up_pre, down_weight, cotangent):
     hbm = pl.BlockSpec(memory_space=pltpu.HBM)
+    vmem = pl.BlockSpec(memory_space=pltpu.VMEM)
     dma = pltpu.SemaphoreType.DMA
     pair = lambda n: [dma((n,)), dma((n,))]
-    return pl.pallas_call(
+    shapes = (
+        jax.ShapeDtypeStruct((OWN, COLS), BF16),
+        jax.ShapeDtypeStruct((HROWS, UNITS), BF16),
+        jax.ShapeDtypeStruct((HROWS, UNITS), BF16),
+        jax.ShapeDtypeStruct((SHARD // 2, COLS), F32),
+    )
+    results = pl.pallas_call(
         kernel,
         name="mlp",
-        out_shape=(
-            jax.ShapeDtypeStruct((OWN, COLS), BF16),
-            jax.ShapeDtypeStruct((HROWS, UNITS), BF16),
-            jax.ShapeDtypeStruct((HROWS, UNITS), BF16),
-            jax.ShapeDtypeStruct((SHARD // 2, COLS), F32),
-        ),
+        out_shape=shapes,
         in_specs=[hbm] * 4,
-        out_specs=(hbm,) * 4,
+        out_specs=(vmem,) * 4,
         scratch_shapes=[
-            pltpu.VMEM((OWN, COLS), BF16),
-            pltpu.VMEM((HROWS, UNITS), BF16),
-            pltpu.VMEM((HROWS, UNITS), BF16),
-            pltpu.VMEM((SHARD // 2, COLS), F32),
             pltpu.VMEM((NCH, HROWS, CH), F32),
             pltpu.VMEM((NCH, HROWS, CH), F32),
             pltpu.VMEM((TOK, UNITS), BF16),
@@ -366,13 +364,21 @@
             pltpu.VMEM((SHARD // 2, COLS), F32),
             pltpu.VMEM((2, SHARD // 2, COLS), BF16),
             pltpu.VMEM((2, SHARD // 2, COLS), BF16),
-            dma((4,)), dma((4,)), *pair(NT), *pair(3 * len(XB)), *pair(NT), *pair(3 * len(HB)), *pair(3 * NCH), *pair(NCH), *pair(3),
+            dma((4,)), *pair(NT), *pair(3 * len(XB)), *pair(NT), *pair(3 * len(HB)), *pair(3 * NCH), *pair(NCH), *pair(3),
             dma, dma, *pair(2),
         ],
         compiler_params=pltpu.CompilerParams(
             collective_id=0, has_side_effects=True, vmem_limit_bytes=60 << 20
         ),
     )(gate_pre, up_pre, down_weight, cotangent)
+    return pl.pallas_call(
+        hand_over,
+        name="results",
+        out_shape=shapes,
+        in_specs=[vmem] * 4,
+        out_specs=(hbm,) * 4,
+        scratch_shapes=[dma((4,))],
+    )(*results)
 
 
 def solution(mesh):

time: 82.4 us -> 78.3 us (0.950)
  local copies, waits for them, and re-layouts: 6.12 us -> 0 us
  Pallas kernels: 75.4 us -> 77.5 us
    unnamed x4 -> x0, local copies, waits for them, and re-layouts: 6.12 us -> none
    pallas_call x1 -> x2, Pallas kernels: 75.4 us -> 77.5 us  [the longest x1 75.6 us: body(): pl.pallas_call(kernel, name='mlp', out_shape=shapes, in_specs=[hbm] * 4,...]
where the time goes in v4:
time: 78.3 us; the launch traced here: 78.1 us
  Pallas kernels  77.5 us (99%)
    pallas_call x1, Pallas kernels, body(): pl.pallas_call(kernel, name='mlp', out_shape=shapes, in_specs=[hbm] * 4,...  75.6 us
    pallas_call x1, Pallas kernels, body(): pl.pallas_call(hand_over, name='results', out_shape=shapes, in_specs=[vme...  1.88 us

profile of v4, /device:TPU:1, one launch (start us, length us, event | category | flops | bytes accessed | tf_op | source)
XLA Modules:
  0.0 78.1 jit_solution(10483164920392593152)
XLA Ops:
  0.6 75.6 %mlp.1 = (bf16[32,512]{1,0:T(8,128)(2,1)}, bf16[16,3584]{1,0:T(8,128)(2,1)}, bf16[16,3584]{1,0:T(8,128)(2,1)}, f32[112,512]{1,0:T(8,128)}) custom-call(bf16[128,3584]{1,0:T(8,128)(2,1)} %gate_in.1, bf16[128,3584]{1,0:T(8,128)(2,1)} %up_in.1, bf16[3584,512]{1,0:T(8,128)(2,1)} %w_in.1, bf16[32,512]{1,0:T(8,128)(2,1)} %cot_in.1), custom_call_target="tpu_custom_call" | custom-call | tf_op jit(solution)/shard_map/mlp/pallas_call | solution.py:340
  76.2 1.9 %results.1 = (bf16[32,512]{1,0:T(8,128)(2,1)}, bf16[16,3584]{1,0:T(8,128)(2,1)}, bf16[16,3584]{1,0:T(8,128)(2,1)}, f32[112,512]{1,0:T(8,128)}) custom-call(bf16[32,512]{1,0:T(8,128)(2,1)} %get-tuple-element.8.a, bf16[16,3584]{1,0:T(8,128)(2,1)} %get-tuple-element.9.b, bf16[16,3584]{1,0:T(8,128)(2,1)} %get-tuple-element.10.c, f32[112,512]{1,0:T(8,128)} %get-tuple-element.11.d), custom_call_target="tpu_custom_call" | custom-call | tf_op jit(solution)/shard_map/results/pallas_call | solution.py:374
